TPU v7x, 128 devices: a whole 4x4x4 slice. The times are simulated.
128 devices in a mesh: wa: 16 (over x, z), ha: 8 (over y, core).
Axes of the slice: x: 4, y: 4, z: 4, core: 2. Of those that a mesh axis runs over, the one named last changes fastest.
Arguments:
- tokens: bfloat16 [512, 16384], P('ha', 'wa'), may hold values from -100 to 100, as said below
- norm_gain: float32 [16384], P('wa'), may hold values from 0.5 to 1.5
- gate_weight: bfloat16 [16384, 26624], P('wa', 'ha'), may hold values from -0.046875 to 0.046875
- up_weight: bfloat16 [16384, 26624], P('wa', 'ha'), may hold values from -0.046875 to 0.046875
- down_weight: bfloat16 [26624, 16384], P('ha', 'wa'), may hold values from -0.0390625 to 0.0390625
Outputs:
- mixed: bfloat16 [512, 16384], P('ha', 'wa')
Inputs may be any that keep to these rules, and one draw needn't show every extreme that they name: `tokens`: real-valued activations.
All inputs are finite; a program needn't handle non-finite values.
Results may differ from a plain program's by a relative error of at most 0.0064.
Values may be sent and summed in bfloat16 or wider, within the bound.
A program may use at most 128 MiB of HBM per device.

v0:
```python
import jax
import jax.numpy as jnp
from jax import lax
from jax.sharding import PartitionSpec as P


def activate(summed, hidden_width, model_width):
    gate = summed[:, :hidden_width]
    up = summed[:, hidden_width : 2 * hidden_width]
    squares = summed[:, 2 * hidden_width : 2 * hidden_width + 1]
    scale = lax.rsqrt(squares / model_width + 1e-05)
    return (jax.nn.silu(gate * scale) * (up * scale)).astype(jnp.bfloat16)


def body(tokens, norm_gain, gate_weight, up_weight, down_weight):
    gathered = lax.all_gather(tokens, "ha", axis=0, tiled=True)
    own_values = gathered.astype(jnp.float32)
    model_width = own_values.shape[1] * lax.axis_size("wa")
    squares = jnp.sum(own_values * own_values, axis=1, keepdims=True)
    scaled = (own_values * norm_gain[None, :]).astype(jnp.bfloat16)
    hidden_width = gate_weight.shape[1]
    gate_part = jnp.dot(scaled, gate_weight, preferred_element_type=jnp.float32)
    up_part = jnp.dot(scaled, up_weight, preferred_element_type=jnp.float32)
    square_block = jnp.broadcast_to(squares, (squares.shape[0], 128))
    summed = lax.psum_scatter(
        jnp.concatenate([gate_part, up_part, square_block], axis=1),
        "wa",
        scatter_dimension=0,
        tiled=True,
    )
    hidden = activate(summed, hidden_width, model_width)
    partial_out = jnp.dot(
        lax.all_gather(hidden, "wa", axis=0, tiled=True),
        down_weight,
        preferred_element_type=jnp.float32,
    )
    mixed_out = lax.psum_scatter(partial_out, "ha", scatter_dimension=0, tiled=True)
    return mixed_out.astype(jnp.bfloat16)


def solution(mesh):
    placed = (P("ha", "wa"), P("wa"), P("wa", "ha"), P("wa", "ha"), P("ha", "wa"))
    return jax.shard_map(body, mesh=mesh, in_specs=placed, out_specs=P("ha", "wa"), check_vma=False)
```

profile of v0, /device:TPU:0, one launch (start us, length us, event | category | flops | bytes accessed | tf_op | source)
XLA Modules:
  0.0 252.2 jit_solution(16157814636659487597)
XLA Ops:
  6.5 0.0 all-gather.3.cloned.1.call-start
  6.5 0.7 all-gather.3.cloned.1.call-update
  7.3 0.0 reduce-scatter.3.cloned.1.call-start
  7.3 27.6 %all-gather.3.cloned.1.call-done = bf16[512,1024]{1,0:T(8,128)(2,1)} async-done(((bf16[64,1024]{1,0:T(8,128)(2,1)}), bf16[512,1024]{1,0:T(8,128)(2,1)}) %all-gather.3.cloned.1.call-update) | async-done | bytes 1048592 | tf_op jit(solution)/shard_map/all_gather | solution.py:16
  34.9 0.0 slice-start
  34.9 1.7 fusion.1
  36.6 0.0 copy-start
  36.6 0.0 slice-start.1
  36.6 0.0 copy-start.1
  36.6 7.3 %fusion.2 = f32[512,3328]{1,0:T(8,128)S(1)} fusion(bf16[1024,3328]{1,0:T(8,128)(2,1)} %param.8, bf16[512,1024]{1,0:T(8,128)(2,1)} %all-gather.3.cloned.1.call-done, f32[1024]{0:T(1024)} %param.6), kind=kOutput, calls=%fused_computation.5 | convolution fusion | flops 3491233792 | bytes 14684160 | tf_op jit(solution)/shard_map/dot_general | solution.py:23
  43.9 0.0 slice-done
  43.9 0.0 copy-done
  43.9 0.0 slice-done.1
  43.9 0.0 copy-done.1
  44.0 3.7 %fusion.4 = f32[512,3328]{1,0:T(8,128)S(1)} fusion(bf16[1024,3328]{1,0:T(8,128)(2,1)S(1)} %bitcast.5, bf16[512,1024]{1,0:T(8,128)(2,1)S(1)} %copy-done, f32[1024]{0:T(1024)S(1)} %copy-done.1), kind=kOutput, calls=%fused_computation.6 | convolution fusion | flops 3491233792 | bytes 14684160 | tf_op jit(solution)/shard_map/dot_general | solution.py:22
  47.7 0.1 broadcast_in_dim.2
  47.8 5.3 %pad_maximum_fusion = f32[512,6784]{1,0:T(8,128)} fusion(f32[512,128]{1,0:T(8,128)S(1)} %broadcast_in_dim.2, f32[512,3328]{1,0:T(8,128)S(1)} %fusion.2, f32[512,3328]{1,0:T(8,128)S(1)} %fusion.4), kind=kLoop, calls=%fused_computation | loop fusion | flops 6946816 | bytes 27787264 | tf_op jit(solution)/shard_map/concatenate | solution.py:26
  53.1 0.0 reduce-scatter.3.cloned.1.call-update
  53.1 0.0 all-gather.5.cloned.1.call-start
  53.1 98.7 %reduce-scatter.3.cloned.1.call-done = f32[32,6784]{1,0:T(8,128)} async-done(((f32[512,6784]{1,0:T(8,128)}), f32[32,6784]{1,0:T(8,128)}) %reduce-scatter.3.cloned.1.call-update) | async-done | bytes 868368 | tf_op jit(solution)/shard_map/reduce_scatter | solution.py:25
  151.8 0.8 fusion.10
  152.6 2.0 fusion.7
  154.7 0.0 all-gather.5.cloned.1.call-update
  154.7 0.0 reduce-scatter.5.cloned.1.call-start
  154.7 47.7 %all-gather.5.cloned.1.call-done = bf16[512,3328]{1,0:T(8,128)(2,1)} async-done(((bf16[32,3328]{1,0:T(8,128)(2,1)}), bf16[512,3328]{1,0:T(8,128)(2,1)}) %all-gather.5.cloned.1.call-update) | async-done | bytes 3407888 | tf_op jit(solution)/shard_map/all_gather | solution.py:33
  202.4 9.0 %fusion.11 = f32[512,1024]{1,0:T(8,128)} fusion(bf16[512,3328]{1,0:T(8,128)(2,1)} %all-gather.5.cloned.1.call-done, bf16[3328,1024]{1,0:T(8,128)(2,1)} %param.9), kind=kOutput, calls=%fused_computation.15 | convolution fusion | flops 3489660928 | bytes 12320768 | tf_op jit(solution)/shard_map/dot_general | solution.py:32
  211.4 0.0 reduce-scatter.5.cloned.1.call-update
  211.5 32.6 %reduce-scatter.5.cloned.1.call-done = f32[64,1024]{1,0:T(8,128)} async-done(((f32[512,1024]{1,0:T(8,128)}), f32[64,1024]{1,0:T(8,128)}) %reduce-scatter.5.cloned.1.call-update) | async-done | bytes 262160 | tf_op jit(solution)/shard_map/reduce_scatter | solution.py:37
  244.0 1.6 convert_element_type.15
  (1 shorter events, 0.0 us)
Async XLA Ops:
  6.5 28.4 %all-gather.3.cloned.1.call-start = ((), (), s32[]{:S(2)}) async-start(), calls=%async_computation.2 | async-start | bytes 1179648 | tf_op jit(solution)/shard_map/all_gather | solution.py:16
  7.3 144.6 %reduce-scatter.3.cloned.1.call-start = ((), (), s32[]{:S(2)}) async-start(), calls=%async_computation.3 | async-start | bytes 14761984 | tf_op jit(solution)/shard_map/reduce_scatter | solution.py:25
  34.9 9.0 %slice-start = ((s8[6815744]{0:T(1024)(128)(4,1)}), s8[4194304]{0:T(1024)(128)(4,1)S(1)}, s32[]{:S(2)}) async-start(s8[6815744]{0:T(1024)(128)(4,1)} %bitcast.4), calls=%async_computation.6 | async-start | bytes 8388608
  36.6 7.3 %copy-start = (bf16[512,1024]{1,0:T(8,128)(2,1)S(1)}, bf16[512,1024]{1,0:T(8,128)(2,1)}, u32[]{:S(2)}) copy-start(bf16[512,1024]{1,0:T(8,128)(2,1)} %all-gather.3.cloned.1.call-done) | copy-start | bytes 3145732
  36.6 7.3 %slice-start.1 = ((s8[6815744]{0:T(1024)(128)(4,1)}), s8[2621440]{0:T(1024)(128)(4,1)S(1)}, s32[]{:S(2)}) async-start(s8[6815744]{0:T(1024)(128)(4,1)} %bitcast.4), calls=%async_computation.7 | async-start | bytes 5242880
  36.6 7.3 %copy-start.1 = (f32[1024]{0:T(1024)S(1)}, f32[1024]{0:T(1024)}, u32[]{:S(2)}) copy-start(f32[1024]{0:T(1024)} %param.6) | copy-start | bytes 12292
  53.1 149.3 %all-gather.5.cloned.1.call-start = ((), (), s32[]{:S(2)}) async-start(), calls=%async_computation.4 | async-start | bytes 3620864 | tf_op jit(solution)/shard_map/all_gather | solution.py:33
  154.7 89.3 %reduce-scatter.5.cloned.1.call-start = ((), (), s32[]{:S(2)}) async-start(), calls=%async_computation.5 | async-start | bytes 2359296 | tf_op jit(solution)/shard_map/reduce_scatter | solution.py:37
Sparse Core Ops, SparseCore 0:
  9.1 25.8 all-gather.2
  53.2 98.5 reduce-scatter.2
  154.8 47.5 all-gather.4
  211.6 32.3 reduce-scatter.4
where the time goes:
time: 252 us
  waiting for transfers between devices  207 us (82%)
  matrix products  20 us (8%)
  between operations  13.2 us (5%)
  other arithmetic  11.4 us (5%)
    reduce_scatter x1, waiting for transfers between devices, body(): lax.psum_scatter(jnp.concatenate([gate_part, up_part, square_block], axis...  98.7 us
    all_gather x1, waiting for transfers between devices, body(): lax.all_gather(hidden, 'wa', axis=0, tiled=True)  47.7 us
    reduce_scatter x1, waiting for transfers between devices, body(): lax.psum_scatter(partial_out, 'ha', scatter_dimension=0, tiled=True)  32.6 us
    all_gather x1, waiting for transfers between devices, body(): gathered = lax.all_gather(tokens, 'ha', axis=0, tiled=True)  27.6 us
    dot_general x1, matrix products, body(): jnp.dot(lax.all_gather(hidden, 'wa', axis=0, tiled=True), down_weight, pr...  9.01 us
    dot_general x1, matrix products, body(): up_part = jnp.dot(scaled, up_weight, preferred_element_type=jnp.float32)  7.28 us
    concatenate x1, other arithmetic, body(): jnp.concatenate([gate_part, up_part, square_block], axis=1)  5.25 us
  transfers between devices with their start and end apart: 4, of which 4 were waited for; matrix products, arithmetic and copies ran while one was open for 0% of the time, Pallas kernels for 0%

commit v1 on v0

--- a/solution.py
+++ b/solution.py
@@ -13,7 +13,11 @@
 
 
 def body(tokens, norm_gain, gate_weight, up_weight, down_weight):
-    gathered = lax.all_gather(tokens, "ha", axis=0, tiled=True)
+    devices = lax.axis_size("ha")
+    repeats = [devices if d == 0 else 1 for d in range(tokens.ndim)]
+    gathered = lax.all_to_all(
+        jnp.tile(tokens, repeats), "ha", split_axis=0, concat_axis=0, tiled=True
+    )
     own_values = gathered.astype(jnp.float32)
     model_width = own_values.shape[1] * lax.axis_size("wa")
     squares = jnp.sum(own_values * own_values, axis=1, keepdims=True)

time: 252 us -> 245 us (0.972)
  waiting for transfers between devices: 207 us -> 180 us
  blocking collectives: 0 us -> 20.5 us
    all_gather x1 -> x0, waiting for transfers between devices: 27.6 us -> none  [body(): gathered = lax.all_gather(tokens, 'ha', axis=0, tiled=True)]
    all_to_all x0 -> x1, blocking collectives: none -> 20.5 us  [body(): lax.all_to_all(jnp.tile(tokens, repeats), 'ha', split_axis=0, concat_axis...]
  transfers between devices with their start and end apart: 4 -> 3, of which waited for: 4 -> 3; matrix products, arithmetic and copies ran while one was open for 0% -> 0% of each run, Pallas kernels for 0% -> 0%
where the time goes in v1:
time: 245 us
  waiting for transfers between devices  180 us (73%)
  blocking collectives  20.5 us (8%)
  matrix products  19 us (8%)
  between operations  13.2 us (5%)
  other arithmetic  11.1 us (5%)
    reduce_scatter x1, waiting for transfers between devices, body(): lax.psum_scatter(jnp.concatenate([gate_part, up_part, square_block], axis...  99.3 us
    all_gather x1, waiting for transfers between devices, body(): lax.all_gather(hidden, 'wa', axis=0, tiled=True)  47.7 us
    reduce_scatter x1, waiting for transfers between devices, body(): lax.psum_scatter(partial_out, 'ha', scatter_dimension=0, tiled=True)  32.6 us
    all_to_all x1, blocking collectives, body(): lax.all_to_all(jnp.tile(tokens, repeats), 'ha', split_axis=0, concat_axis...  20.5 us
    dot_general x1, matrix products, body(): jnp.dot(lax.all_gather(hidden, 'wa', axis=0, tiled=True), down_weight, pr...  9.01 us
    dot_general x1, matrix products, body(): up_part = jnp.dot(scaled, up_weight, preferred_element_type=jnp.float32)  6.34 us
    concatenate x1, other arithmetic, body(): jnp.concatenate([gate_part, up_part, square_block], axis=1)  5.24 us
  transfers between devices with their start and end apart: 3, of which 3 were waited for; matrix products, arithmetic and copies ran while one was open for 0% of the time, Pallas kernels for 0%

profile of v1, /device:TPU:0, one launch (start us, length us, event | category | flops | bytes accessed | tf_op | source)
XLA Modules:
  0.0 244.6 jit_solution(1070338222243900285)
XLA Ops:
  6.5 0.0 reduce-scatter.3.cloned.1.call-start
  6.5 1.0 tile.2
  7.6 20.5 %all_to_all.6 = bf16[8,64,1024]{2,1,0:T(8,128)(2,1)S(1)} all-to-all(bf16[8,64,1024]{2,1,0:T(8,128)(2,1)S(1)} %tile.2), channel_id=1, replica_groups=mesh['wa'=16,'ha'=8] {'ha'}, dimensions={0} | all-to-all | bytes 2097152 | tf_op jit(solution)/shard_map/all_to_all | solution.py:18
  28.0 0.3 multiply_reduce_fusion
  28.3 0.1 broadcast_in_dim.4
  28.4 0.0 slice-start
  28.4 1.1 fusion
  29.4 0.0 slice-start.1
  29.5 6.3 %fusion.7 = f32[512,3328]{1,0:T(8,128)S(1)} fusion(bf16[512,1024]{1,0:T(8,128)(2,1)S(1)} %fusion, bf16[1024,3328]{1,0:T(8,128)(2,1)} %param.8), kind=kOutput, calls=%fused_computation.13 | convolution fusion | flops 3489660928 | bytes 14680064 | tf_op jit(solution)/shard_map/dot_general | solution.py:27
  35.8 0.0 slice-done
  35.8 0.0 slice-done.1
  35.8 3.7 %fusion.6 = f32[512,3328]{1,0:T(8,128)S(1)} fusion(bf16[512,1024]{1,0:T(8,128)(2,1)S(1)} %fusion, bf16[1024,3328]{1,0:T(8,128)(2,1)S(1)} %bitcast.11), kind=kOutput, calls=%fused_computation.12 | convolution fusion | flops 3489660928 | bytes 14680064 | tf_op jit(solution)/shard_map/dot_general | solution.py:26
  39.5 0.1 broadcast_in_dim.10
  39.7 5.2 %pad_maximum_fusion = f32[512,6784]{1,0:T(8,128)} fusion(f32[512,128]{1,0:T(8,128)S(1)} %broadcast_in_dim.10, f32[512,3328]{1,0:T(8,128)S(1)} %fusion.7, f32[512,3328]{1,0:T(8,128)S(1)} %fusion.6), kind=kLoop, calls=%fused_computation | loop fusion | flops 6946816 | bytes 27787264 | tf_op jit(solution)/shard_map/concatenate | solution.py:30
  44.9 0.0 reduce-scatter.3.cloned.1.call-update
  44.9 0.0 all-gather.2.cloned.1.call-start
  45.0 99.3 %reduce-scatter.3.cloned.1.call-done = f32[32,6784]{1,0:T(8,128)} async-done(((f32[512,6784]{1,0:T(8,128)}), f32[32,6784]{1,0:T(8,128)}) %reduce-scatter.3.cloned.1.call-update) | async-done | bytes 868368 | tf_op jit(solution)/shard_map/reduce_scatter | solution.py:29
  144.2 0.8 fusion.5
  145.1 2.0 fusion.2
  147.1 0.0 all-gather.2.cloned.1.call-update
  147.1 0.0 reduce-scatter.5.cloned.1.call-start
  147.2 47.7 %all-gather.2.cloned.1.call-done = bf16[512,3328]{1,0:T(8,128)(2,1)} async-done(((bf16[32,3328]{1,0:T(8,128)(2,1)}), bf16[512,3328]{1,0:T(8,128)(2,1)}) %all-gather.2.cloned.1.call-update) | async-done | bytes 3407888 | tf_op jit(solution)/shard_map/all_gather | solution.py:37
  194.9 9.0 %fusion.8 = f32[512,1024]{1,0:T(8,128)} fusion(bf16[512,3328]{1,0:T(8,128)(2,1)} %all-gather.2.cloned.1.call-done, bf16[3328,1024]{1,0:T(8,128)(2,1)} %param.9), kind=kOutput, calls=%fused_computation.14 | convolution fusion | flops 3489660928 | bytes 12320768 | tf_op jit(solution)/shard_map/dot_general | solution.py:36
  203.9 0.0 reduce-scatter.5.cloned.1.call-update
  203.9 32.6 %reduce-scatter.5.cloned.1.call-done = f32[64,1024]{1,0:T(8,128)} async-done(((f32[512,1024]{1,0:T(8,128)}), f32[64,1024]{1,0:T(8,128)}) %reduce-scatter.5.cloned.1.call-update) | async-done | bytes 262160 | tf_op jit(solution)/shard_map/reduce_scatter | solution.py:41
  236.5 1.6 convert_element_type.23
  (1 shorter events, 0.0 us)
Async XLA Ops:
  6.5 137.7 %reduce-scatter.3.cloned.1.call-start = ((), (), s32[]{:S(2)}) async-start(), calls=%async_computation.3 | async-start | bytes 14761984 | tf_op jit(solution)/shard_map/reduce_scatter | solution.py:29
  28.4 7.4 %slice-start = ((s8[6815744]{0:T(1024)(128)(4,1)}), s8[4194304]{0:T(1024)(128)(4,1)S(1)}, s32[]{:S(2)}) async-start(s8[6815744]{0:T(1024)(128)(4,1)} %bitcast.10), calls=%async_computation.6 | async-start | bytes 8388608
  29.4 6.4 %slice-start.1 = ((s8[6815744]{0:T(1024)(128)(4,1)}), s8[2621440]{0:T(1024)(128)(4,1)S(1)}, s32[]{:S(2)}) async-start(s8[6815744]{0:T(1024)(128)(4,1)} %bitcast.10), calls=%async_computation.7 | async-start | bytes 5242880
  44.9 150.0 %all-gather.2.cloned.1.call-start = ((), (), s32[]{:S(2)}) async-start(), calls=%async_computation.4 | async-start | bytes 3620864 | tf_op jit(solution)/shard_map/all_gather | solution.py:37
  147.1 89.4 %reduce-scatter.5.cloned.1.call-start = ((), (), s32[]{:S(2)}) async-start(), calls=%async_computation.5 | async-start | bytes 2359296 | tf_op jit(solution)/shard_map/reduce_scatter | solution.py:41
Sparse Core Ops, SparseCore 0:
  45.0 99.1 reduce-scatter.2
  147.2 47.5 all-gather.1
  204.0 32.3 reduce-scatter.4
